TPU v7x, 256 devices: a whole 4x4x8 slice. The times are simulated.
256 devices in a mesh: ctx: 32 (over y, z), head: 8 (over x, core).
Axes of the slice: x: 4, y: 4, z: 8, core: 2. Of those that a mesh axis runs over, the one named last changes fastest.
Arguments:
- queries: bfloat16 [8192, 4096], P('ctx', 'head'), may hold values from -6 to 6
- key_rows: bfloat16 [8192, 4096], P('ctx', 'head'), may hold values from -0.5 to 0.5
- value_rows: bfloat16 [8192, 4096], P('ctx', 'head'), may hold values from -6 to 6
- doc_ids: int32 [8192], P('ctx'), may hold values from 0 to 15, never falling along the last dimension, each value on 1 to 2048 neighbouring positions
- out_grad: bfloat16 [8192, 6144], P(('ctx', 'head')), may hold values from -6 to 6
- out_weight: bfloat16 [4096, 6144], P('head', 'ctx'), may hold values from -0.09375 to 0.09375
Outputs:
- layer_out: bfloat16 [8192, 6144], P(('ctx', 'head'))
- query_grad: bfloat16 [8192, 4096], P('ctx', 'head')
- key_grad: bfloat16 [8192, 4096], P('ctx', 'head')
- value_grad: bfloat16 [8192, 4096], P('ctx', 'head')
- weight_grad: bfloat16 [4096, 6144], P(('head', 'ctx'))
Inputs may be any that keep to these rules, and one draw needn't show every extreme that they name: `doc_ids`: repository ids never fall along the sequence; each repository covers 1 to 2048 tokens, and one covers exactly that many.
All inputs are finite; a program needn't handle non-finite values.
Results may differ from a plain program's by a relative error of at most 0.025.
Values may be sent and summed in bfloat16 or wider, within the bound.
No kernel may reach another device: no remote copies, remote signals or barrier semaphores. Data moves between devices by JAX's collectives and lax.ppermute only.
A program may use at most 128 MiB of HBM per device.

v0:
```python
import jax
import jax.numpy as jnp
from jax import lax
from jax.sharding import PartitionSpec as P

HD = 128
EPSILON = 1e-05


def carried_in(x, axis, join, neutral, backward):
    count = lax.axis_size(axis)
    place = lax.axis_index(axis)
    ahead = count - 1 - place if backward else place
    gathered = jax.tree.map(
        lambda a, kind: lax.all_gather(a.astype(kind), axis),
        x,
        (jnp.bfloat16, jnp.bfloat16, jnp.bfloat16),
    )
    state = jax.tree.map(lambda a, e: jnp.zeros_like(a) + jnp.asarray(e, a.dtype), x, neutral)

    def one(lap, state):
        source = count - 1 - lap if backward else lap
        return join(
            state,
            jax.tree.map(
                lambda a, own: lax.dynamic_index_in_dim(a, source, 0, False).astype(own.dtype),
                gathered,
                x,
            ),
        )

    return lax.fori_loop(0, ahead, one, state)


def forward_link(earlier_part, later_part):
    early_first, early_last, early_state = earlier_part
    late_first, late_last, late_state = later_part
    late_empty = late_last < 0.0
    early_empty = early_last < 0.0
    linked = (early_last == late_first) & (late_first == late_last)
    joined = late_state + jnp.where(linked, early_state, jnp.float32(0.0))
    return (
        jnp.where(early_empty, late_first, early_first),
        jnp.where(late_empty, early_last, late_last),
        jnp.where(late_empty, early_state, joined),
    )


def backward_link(earlier_part, later_part):
    high_first, high_last, high_state = earlier_part
    low_first, low_last, low_state = later_part
    low_empty = low_last < 0.0
    high_empty = high_last < 0.0
    linked = (high_first == low_last) & (low_first == low_last)
    joined = low_state + jnp.where(linked, high_state, jnp.float32(0.0))
    return (
        jnp.where(low_empty, high_first, low_first),
        jnp.where(high_empty, low_last, high_last),
        jnp.where(low_empty, high_state, joined),
    )


def shards(queries, key_rows, value_rows, doc_ids, out_grad, out_weight):
    tok_count, full_width = queries.shape
    head_count = full_width // HD
    query_heads = queries.reshape(tok_count, head_count, HD)
    key_heads = key_rows.reshape(tok_count, head_count, HD)
    value_heads = value_rows.reshape(tok_count, head_count, HD)
    doc_values = doc_ids.astype(jnp.float32)
    first_doc = doc_values[:1]
    last_doc = doc_values[-1:]
    causal = jnp.tril(jnp.ones((tok_count, tok_count), dtype=bool))
    allowed = (causal & (doc_ids[:, None] == doc_ids[None, :]))[None]
    scores = jnp.einsum("thd,shd->hts", query_heads, key_heads, preferred_element_type=jnp.float32)
    weights = jnp.where(allowed, scores, jnp.float32(0.0)).astype(jnp.bfloat16)
    key_last = jnp.where(
        (doc_values == last_doc)[:, None, None], key_heads, jnp.zeros_like(key_heads)
    )
    local_state = jnp.einsum(
        "thd,the->hde", key_last, value_heads, preferred_element_type=jnp.float32
    )
    empty_marks = jnp.full((1,), -1.0, jnp.float32)
    identity = (empty_marks, empty_marks, jnp.zeros_like(local_state))
    prior_first, prior_last, prior_state = carried_in(
        (first_doc, last_doc, local_state), "ctx", forward_link, identity, False
    )
    row_mask = doc_values == prior_last
    prior_rounded = prior_state.astype(jnp.bfloat16)
    inter = jnp.einsum(
        "thd,hde->the", query_heads, prior_rounded, preferred_element_type=jnp.float32
    )
    mixed = jnp.einsum(
        "hts,she->the", weights, value_heads, preferred_element_type=jnp.float32
    ) + jnp.where(row_mask[:, None, None], inter, jnp.float32(0.0))
    inv_norm = lax.rsqrt(jnp.mean(mixed * mixed, axis=-1, keepdims=True) + EPSILON)
    normed = mixed * inv_norm
    normed_flat = normed.astype(jnp.bfloat16).reshape(tok_count, full_width)
    full_weight = lax.all_gather(out_weight, "ctx", axis=1, tiled=True)
    layer_out = lax.psum_scatter(
        jnp.dot(normed_flat, full_weight, preferred_element_type=jnp.float32).astype(jnp.bfloat16),
        "head",
        scatter_dimension=0,
        tiled=True,
    )
    grad_full = lax.all_gather(out_grad, "head", axis=0, tiled=True)
    grad_normed = lax.dot_general(
        grad_full, full_weight, (((1,), (1,)), ((), ())), preferred_element_type=jnp.float32
    ).reshape(tok_count, head_count, HD)
    mixed_grad = (
        inv_norm * (grad_normed - normed * jnp.mean(grad_normed * normed, axis=-1, keepdims=True))
    ).astype(jnp.bfloat16)
    weight_grad = lax.psum_scatter(
        lax.dot_general(
            normed_flat, grad_full, (((0,), (0,)), ((), ())), preferred_element_type=jnp.float32
        ).astype(jnp.bfloat16),
        "ctx",
        scatter_dimension=0,
        tiled=True,
    )
    query_first = jnp.where(
        (doc_values == first_doc)[:, None, None], query_heads, jnp.zeros_like(query_heads)
    )
    local_future = jnp.einsum(
        "thd,the->hde", query_first, mixed_grad, preferred_element_type=jnp.float32
    )
    later_first, later_last, future_state = carried_in(
        (first_doc, last_doc, local_future), "ctx", backward_link, identity, True
    )
    col_mask = (doc_values == later_first)[:, None, None]
    future_rounded = future_state.astype(jnp.bfloat16)
    grad_raw = jnp.einsum(
        "the,she->hts", mixed_grad, value_heads, preferred_element_type=jnp.float32
    )
    grad_scores = jnp.where(allowed, grad_raw, jnp.float32(0.0)).astype(jnp.bfloat16)
    query_grad = jnp.einsum(
        "hts,shd->thd", grad_scores, key_heads, preferred_element_type=jnp.float32
    ) + jnp.where(
        row_mask[:, None, None],
        jnp.einsum("the,hde->thd", mixed_grad, prior_rounded, preferred_element_type=jnp.float32),
        jnp.float32(0.0),
    )
    key_grad = jnp.einsum(
        "hts,thd->shd", grad_scores, query_heads, preferred_element_type=jnp.float32
    ) + jnp.where(
        col_mask,
        jnp.einsum("she,hde->shd", value_heads, future_rounded, preferred_element_type=jnp.float32),
        jnp.float32(0.0),
    )
    value_grad = jnp.einsum(
        "hts,the->she", weights, mixed_grad, preferred_element_type=jnp.float32
    ) + jnp.where(
        col_mask,
        jnp.einsum("shd,hde->she", key_heads, future_rounded, preferred_element_type=jnp.float32),
        jnp.float32(0.0),
    )
    return (
        layer_out,
        query_grad.astype(jnp.bfloat16).reshape(tok_count, full_width),
        key_grad.astype(jnp.bfloat16).reshape(tok_count, full_width),
        value_grad.astype(jnp.bfloat16).reshape(tok_count, full_width),
        weight_grad,
    )


def solution(mesh):
    return jax.shard_map(
        shards,
        mesh=mesh,
        in_specs=(
            P("ctx", "head"),
            P("ctx", "head"),
            P("ctx", "head"),
            P("ctx"),
            P(("ctx", "head"), None),
            P("head", "ctx"),
        ),
        out_specs=(
            P(("ctx", "head"), None),
            P("ctx", "head"),
            P("ctx", "head"),
            P("ctx", "head"),
            P(("head", "ctx"), None),
        ),
        check_vma=False,
    )
```

profile of v0, /device:TPU:2, one launch (start us, length us, event | category | flops | bytes accessed | tf_op | source)
XLA Modules:
  0.0 609.2 jit_solution(14436302235198908007)
XLA Ops:
  7.2 0.7 convert_element_type.105
  7.9 1.1 copy.86
  9.6 2.0 broadcast_compare_fusion.1
  11.6 0.9 convolution_convert_fusion.3
  12.5 0.7 all-gather.11.cloned.1.call-update
  13.3 0.7 all-gather.9.cloned.1.call-update
  14.0 1.3 dynamic-slice
  15.9 1.4 dynamic-update-slice
  17.3 1.4 dynamic-update-slice.1
  18.7 78.3 %all-reduce.2 = (bf16[32]{0:T(256)(128)(2,1)S(1)}, bf16[32]{0:T(256)(128)(2,1)S(1)}) all-reduce(bf16[32]{0:T(256)(128)(2,1)S(1)} %dynamic-update-slice, bf16[32]{0:T(256)(128)(2,1)S(1)} %dynamic-update-slice.1), channel_id=2, replica_groups=mesh['ctx'=32,'head'=8] {'ctx'}, use_global_device_ids=true, to_apply=%add | all-reduce | flops 64 | bytes 256
  97.0 1.1 copy.59
  98.1 0.9 fusion.22
  99.0 1.3 fusion.2
  101.0 24.8 %all-gather.11.cloned.1.call-done = bf16[256,6144]{1,0:T(8,128)(2,1)} async-done(((bf16[32,6144]{1,0:T(8,128)(2,1)}), bf16[256,6144]{1,0:T(8,128)(2,1)}) %all-gather.11.cloned.1.call-update) | async-done | bytes 3145744 | tf_op jit(solution)/shard_map/all_gather | solution.py:105
  125.8 92.5 %all-gather.9.cloned.1.call-done = bf16[512,6144]{0,1:T(8,128)(2,1)} async-done(((bf16[512,192]{0,1:T(8,128)(2,1)}), bf16[512,6144]{0,1:T(8,128)(2,1)}) %all-gather.9.cloned.1.call-update) | async-done | bytes 6291472 | tf_op jit(solution)/shard_map/all_gather | solution.py:98
  218.2 6.3 %multiply_reduce_fusion = (f32[256,4]{0,1:T(4,128)S(1)}, f32[256,512]{0,1:T(8,128)S(1)}) fusion(f32[256,4,128]{0,2,1:T(8,128)S(1)} %get-tuple-element.234, f32[256,4]{0,1:T(4,128)S(1)} %add_rsqrt_fusion, bf16[256,6144]{1,0:T(8,128)(2,1)} %all-gather.11.cloned.1.call-done, bf16[512,6144]{0,1:T(8,128)(2,1)} %all-gather.9.cloned.1.call-done), kind=kOutput, calls=%fused_computation.34 | convolution fusion | flops 1611004928 | bytes 10493952 | tf_op jit(solution)/shard_map/dot_general | solution.py:106
  224.7 0.9 convolution_convert_fusion.2
  225.6 6.4 %convolution_convert_fusion.1 = bf16[256,6144]{1,0:T(8,128)(2,1)} fusion(bf16[256,512]{0,1:T(8,128)(2,1)S(1)} %bitcast.132, bf16[512,6144]{0,1:T(8,128)(2,1)} %all-gather.9.cloned.1.call-done), kind=kOutput, calls=%fused_computation.9 | convolution fusion | flops 1612185600 | bytes 9699328 | tf_op jit(solution)/shard_map/dot_general | solution.py:100
  232.1 6.4 %convolution_convert_fusion = bf16[512,6144]{1,0:T(8,128)(2,1)} fusion(bf16[256,512]{0,1:T(8,128)(2,1)S(1)} %bitcast.133, bf16[256,6144]{1,0:T(8,128)(2,1)} %all-gather.11.cloned.1.call-done), kind=kOutput, calls=%fused_computation.8 | convolution fusion | flops 1613758464 | bytes 9699328 | tf_op jit(solution)/shard_map/dot_general | solution.py:113
  239.4 0.8 copy.50
  240.7 94.9 %all-gather.15.cloned.1.call-done = bf16[128,128,128]{2,1,0:T(8,128)(2,1)} async-done(((bf16[4,128,128]{2,1,0:T(8,128)(2,1)}), bf16[128,128,128]{2,1,0:T(8,128)(2,1)}) %all-gather.15.cloned.1.call-update) | async-done | bytes 4194320 | tf_op jit(solution)/shard_map/all_gather | solution.py:15
  335.7 158.6 %while.31 = (s32[]{:T(128)}, f32[1]{0:T(128)}, f32[4,128,128]{2,1,0:T(8,128)S(1)}, s32[]{:T(128)}, bf16[32,1]{0,1:T(2,128)(2,1)S(1)}, /*index=5*/bf16[32,1]{0,1:...) while((s32[]{:T(128)}, f32[1]{0:T(128)}, ...), condition=%wide.region_6.7_spmd, body=%wide.region_5.6_spmd.sunk | while | flops 262155 | bytes 655590 | solution.py:32
  335.7 0.7 constant_dynamic-slice_fusion.7
  339.7 1.0 fusion.69
  340.8 0.7 constant_dynamic-slice_fusion.7
  344.8 1.0 fusion.69
  345.9 0.7 constant_dynamic-slice_fusion.7
  350.0 1.0 fusion.69
  351.0 0.7 constant_dynamic-slice_fusion.7
  355.1 1.0 fusion.69
  360.2 1.0 fusion.69
  365.3 1.0 fusion.69
  366.4 0.7 constant_dynamic-slice_fusion.7
  370.4 1.0 fusion.69
  371.5 0.7 constant_dynamic-slice_fusion.7
  375.5 1.0 fusion.69
  376.6 0.7 constant_dynamic-slice_fusion.7
  380.7 1.0 fusion.69
  385.8 1.0 fusion.69
  386.8 0.7 constant_dynamic-slice_fusion.7
  390.9 1.0 fusion.69
  396.0 1.0 fusion.69
  401.1 1.0 fusion.69
  406.2 1.0 fusion.69
  411.3 1.0 fusion.69
  416.5 1.0 fusion.69
  421.6 1.0 fusion.69
  426.7 1.0 fusion.69
  431.8 1.0 fusion.69
  436.9 1.0 fusion.69
  442.0 1.1 fusion.69
  447.2 1.0 fusion.69
  452.3 1.0 fusion.69
  457.4 1.0 fusion.69
  462.5 1.0 fusion.69
  467.6 1.0 fusion.69
  472.7 1.0 fusion.69
  477.9 1.0 fusion.69
  483.0 1.0 fusion.69
  488.1 1.0 fusion.69
  493.2 1.0 fusion.69
  494.5 0.8 copy.51
  495.6 0.8 copy.52
  496.5 105.9 %reduce-scatter.5.cloned.1.call-done = bf16[16,6144]{1,0:T(8,128)(2,1)} async-done(((bf16[512,6144]{1,0:T(8,128)(2,1)}), bf16[16,6144]{1,0:T(8,128)(2,1)}) %reduce-scatter.5.cloned.1.call-update) | async-done | bytes 196624 | tf_op jit(solution)/shard_map/reduce_scatter | solution.py:112
  (62 shorter events, 19.5 us)
Async XLA Ops:
  7.2 4.4 copy-start
  7.2 93.4 %all-gather.13.cloned.1.call-start = ((), (), s32[]{:S(2)}) async-start(), calls=%async_computation.6 | async-start | bytes 4325376 | tf_op jit(solution)/shard_map/all_gather | solution.py:15
  11.6 89.1 %copy-start.2 = (s32[256]{0:T(256)S(1)}, s32[256]{0:T(256)}, u32[]{:S(2)}) copy-start(s32[256]{0:T(256)} %param.13) | copy-start | bytes 3076
  12.5 113.3 %all-gather.11.cloned.1.call-start = ((), (), s32[]{:S(2)}) async-start(), calls=%async_computation.4 | async-start | bytes 3538944 | tf_op jit(solution)/shard_map/all_gather | solution.py:105
  13.2 205.0 %all-gather.9.cloned.1.call-start = ((), (), s32[]{:S(2)}) async-start(), calls=%async_computation.2 | async-start | bytes 6488064 | tf_op jit(solution)/shard_map/all_gather | solution.py:98
  14.0 321.7 %all-gather.15.cloned.1.call-start = ((), (), s32[]{:S(2)}) async-start(), calls=%async_computation.7 | async-start | bytes 4325376 | tf_op jit(solution)/shard_map/all_gather | solution.py:15
  225.6 270.9 %reduce-scatter.3.cloned.1.call-start = ((), (), s32[]{:S(2)}) async-start(), calls=%async_computation.3 | async-start | bytes 3538944 | tf_op jit(solution)/shard_map/reduce_scatter | solution.py:99
  232.1 370.3 %reduce-scatter.5.cloned.1.call-start = ((), (), s32[]{:S(2)}) async-start(), calls=%async_computation.5 | async-start | bytes 6488064 | tf_op jit(solution)/shard_map/reduce_scatter | solution.py:112
  240.2 255.1 %copy-start.1 = (bf16[256,512]{1,0:T(8,128)(2,1)S(1)}, bf16[256,512]{1,0:T(8,128)(2,1)}, u32[]{:S(2)}) copy-start(bf16[256,512]{1,0:T(8,128)(2,1)} %param.11) | copy-start | bytes 786436
Sparse Core Ops, SparseCore 0:
  12.6 84.7 all-gather.12
  99.3 26.4 all-gather.10
  128.3 89.8 all-gather.8
  225.7 109.8 all-gather.14
  338.6 32.1 reduce-scatter.2
  375.2 227.1 reduce-scatter.4
where the time goes:
time: 612 us; the launch traced here: 609 us
  waiting for transfers between devices  320 us (52%)
  loops' own time  105 us (17%)
  blocking collectives  78.3 us (13%)
  other arithmetic  36.1 us (6%)
  local copies, waits for them, and re-layouts  30.8 us (5%)
  matrix products  24.5 us (4%)
  between operations  14.3 us (2%)
    reduce_scatter x1, waiting for transfers between devices, shards(): lax.psum_scatter(lax.dot_general(normed_flat, grad_full, (((0,), (0,)), (...  106 us
    another operation x2, loops' own time, carried_in(): return lax.fori_loop(0, ahead, one, state)  105 us
    all_gather x2, waiting for transfers between devices, carried_in(): lax.all_gather(a.astype(kind), axis)  95 us
    all_gather x1, waiting for transfers between devices, shards(): full_weight = lax.all_gather(out_weight, 'ctx', axis=1, tiled=True)  92.5 us
    unnamed x1, blocking collectives  78.3 us
    select_n x31, other arithmetic, backward_link(): jnp.where(low_empty, high_state, joined)  32.4 us
    all_gather x1, waiting for transfers between devices, shards(): grad_full = lax.all_gather(out_grad, 'head', axis=0, tiled=True)  24.8 us
    dynamic_slice x31, local copies, waits for them, and re-layouts, one(): lax.dynamic_index_in_dim(a, source, 0, False).astype(own.dtype)  20.8 us
  transfers between devices with their start and end apart: 6, of which 4 were waited for; matrix products, arithmetic and copies ran while one was open for 13% of the time, Pallas kernels for 0%

commit v1 on v0

--- a/solution.py
+++ b/solution.py
@@ -5,6 +5,24 @@
 
 HD = 128
 EPSILON = 1e-05
+
+
+def gather_around(value, axis, dim):
+    ways, here, turn = (lax.axis_size(axis), lax.axis_index(axis), value.shape[dim])
+    dims = [n * ways if d == dim else n for d, n in enumerate(value.shape)]
+    full = lax.dynamic_update_slice_in_dim(
+        jnp.zeros(dims, value.dtype), value, here * turn, axis=dim
+    )
+    going_up = going_down = value
+    for far in range(1, ways // 2 + 1):
+        going_up = lax.ppermute(going_up, axis, [(d, (d + 1) % ways) for d in range(ways)])
+        full = lax.dynamic_update_slice_in_dim(full, going_up, (here - far) % ways * turn, axis=dim)
+        if 2 * far < ways:
+            going_down = lax.ppermute(going_down, axis, [(d, (d - 1) % ways) for d in range(ways)])
+            full = lax.dynamic_update_slice_in_dim(
+                full, going_down, (here + far) % ways * turn, axis=dim
+            )
+    return full
 
 
 def carried_in(x, axis, join, neutral, backward):
@@ -102,7 +120,7 @@
         scatter_dimension=0,
         tiled=True,
     )
-    grad_full = lax.all_gather(out_grad, "head", axis=0, tiled=True)
+    grad_full = gather_around(out_grad, "head", 0)
     grad_normed = lax.dot_general(
         grad_full, full_weight, (((1,), (1,)), ((), ())), preferred_element_type=jnp.float32
     ).reshape(tok_count, head_count, HD)

time: 612 us -> 662 us (1.082)
  waiting for transfers between devices: 320 us -> 363 us
    all_gather x2, waiting for transfers between devices: 95 us -> 177 us  [carried_in(): lax.all_gather(a.astype(kind), axis)]
    all_gather x1, waiting for transfers between devices: 92.5 us -> 57.6 us  [shards(): full_weight = lax.all_gather(out_weight, 'ctx', axis=1, tiled=True)]
    all_gather x1 -> x0, waiting for transfers between devices: 24.8 us -> none  [shards(): grad_full = lax.all_gather(out_grad, 'head', axis=0, tiled=True)]
    ppermute x0 -> x7, waiting for transfers between devices: none -> 15.8 us  [the longest x4 15.7 us: gather_around(): lax.ppermute(going_up, axis, [(d, (d + 1) % ways) for d in range(ways)])]
  transfers between devices with their start and end apart: 6 -> 12, of which waited for: 4 -> 7; matrix products, arithmetic and copies ran while one was open for 13% -> 12% of each run, Pallas kernels for 0% -> 0%
where the time goes in v1:
time: 662 us; the launch traced here: 660 us
  waiting for transfers between devices  363 us (55%)
  loops' own time  102 us (15%)
  blocking collectives  78.3 us (12%)
  other arithmetic  36.8 us (6%)
  local copies, waits for them, and re-layouts  34 us (5%)
  matrix products  25.6 us (4%)
  between operations  14.2 us (2%)
    all_gather x2, waiting for transfers between devices, carried_in(): lax.all_gather(a.astype(kind), axis)  177 us
    reduce_scatter x1, waiting for transfers between devices, shards(): lax.psum_scatter(lax.dot_general(normed_flat, grad_full, (((0,), (0,)), (...  112 us
    another operation x2, loops' own time, carried_in(): return lax.fori_loop(0, ahead, one, state)  102 us
    unnamed x1, blocking collectives  78.3 us
    all_gather x1, waiting for transfers between devices, shards(): full_weight = lax.all_gather(out_weight, 'ctx', axis=1, tiled=True)  57.6 us
    select_n x31, other arithmetic, backward_link(): jnp.where(low_empty, high_state, joined)  32.4 us
    dynamic_slice x31, local copies, waits for them, and re-layouts, one(): lax.dynamic_index_in_dim(a, source, 0, False).astype(own.dtype)  18.4 us
    ppermute x4, waiting for transfers between devices, gather_around(): lax.ppermute(going_up, axis, [(d, (d + 1) % ways) for d in range(ways)])  15.7 us
  transfers between devices with their start and end apart: 12, of which 7 were waited for; matrix products, arithmetic and copies ran while one was open for 12% of the time, Pallas kernels for 0%

profile of v1, /device:TPU:2, one launch (start us, length us, event | category | flops | bytes accessed | tf_op | source)
XLA Modules:
  0.0 659.7 jit_solution(11807138588603772672)
XLA Ops:
  7.9 1.1 copy.86
  9.6 2.0 broadcast_compare_fusion.1
  11.6 0.9 convolution_convert_fusion.3
  13.3 1.3 dynamic-slice
  15.2 1.4 dynamic-update-slice
  16.6 1.4 dynamic-update-slice.1
  18.0 1.7 collective-permute-start.1
  19.7 78.3 %all-reduce.2 = (bf16[32]{0:T(256)(128)(2,1)S(1)}, bf16[32]{0:T(256)(128)(2,1)S(1)}) all-reduce(bf16[32]{0:T(256)(128)(2,1)S(1)} %dynamic-update-slice, bf16[32]{0:T(256)(128)(2,1)S(1)} %dynamic-update-slice.1), channel_id=2, replica_groups=mesh['ctx'=32,'head'=8] {'ctx'}, use_global_device_ids=true, to_apply=%add | all-reduce | flops 64 | bytes 256
  98.1 1.8 copy.59
  99.9 0.9 fusion.22
  101.2 1.3 fusion.2
  102.5 1.1 convolution_bitcast_fusion.2
  103.7 1.7 collective-permute-start.3
  105.4 1.0 constant_dynamic-update-slice_fusion.6
  106.4 1.0 constant_dynamic-update-slice_fusion.5
  107.5 3.6 collective-permute-done.2
  111.1 2.0 collective-permute-start.5
  113.2 5.1 collective-permute-done.4
  118.4 7.0 %collective-permute-done.6 = bf16[32,6144]{1,0:T(8,128)(2,1)S(1)} collective-permute-done((bf16[32,6144]{1,0:T(8,128)(2,1)S(1)}, bf16[32,6144]{1,0:T(8,128)(2,1)S(1)}, u32[]{:S(2)}, u32[]{:S(2)}) %collective-permute-start.6) | collective-permute-done | bytes 393248 | tf_op jit(solution)/shard_map/ppermute | solution.py:18
  126.3 2.3 multiply_reduce_fusion.1
  128.6 57.6 %all-gather.8.cloned.1.call-done = bf16[512,6144]{0,1:T(8,128)(2,1)} async-done(((bf16[512,192]{0,1:T(8,128)(2,1)}), bf16[512,6144]{0,1:T(8,128)(2,1)}) %all-gather.8.cloned.1.call-update) | async-done | bytes 6291472 | tf_op jit(solution)/shard_map/all_gather | solution.py:116
  186.1 5.5 multiply_reduce_fusion
  191.6 0.8 multiply_convert_fusion
  193.2 0.9 convolution_convert_fusion.2
  194.1 6.5 convolution_convert_fusion.1
  200.7 5.4 convolution_convert_fusion
  206.1 0.9 copy-done.4
  207.9 0.8 copy.50
  209.3 177.0 %all-gather.12.cloned.1.call-done = bf16[128,128,128]{2,1,0:T(8,128)(2,1)} async-done(((bf16[4,128,128]{2,1,0:T(8,128)(2,1)}), bf16[128,128,128]{2,1,0:T(8,128)(2,1)}) %all-gather.12.cloned.1.call-update) | async-done | bytes 4194320 | tf_op jit(solution)/shard_map/all_gather | solution.py:33
  386.3 152.5 %while.31 = (s32[]{:T(128)}, f32[1]{0:T(128)}, f32[4,128,128]{2,1,0:T(8,128)S(1)}, s32[]{:T(128)}, bf16[32,1]{0,1:T(2,128)(2,1)S(1)}, /*index=5*/bf16[32,1]{0,1:...) while((s32[]{:T(128)}, f32[1]{0:T(128)}, ...), condition=%wide.region_6.7_spmd, body=%wide.region_5.6_spmd.sunk | while | flops 262155 | bytes 655590 | solution.py:50
  390.2 1.0 fusion.69
  395.1 1.0 fusion.69
  400.0 1.0 fusion.69
  405.0 1.0 fusion.69
  409.9 1.0 fusion.69
  414.8 1.0 fusion.69
  419.7 1.0 fusion.69
  424.6 1.0 fusion.69
  429.6 1.0 fusion.69
  434.5 1.0 fusion.69
  439.4 1.1 fusion.69
  444.3 1.0 fusion.69
  449.2 1.0 fusion.69
  454.2 1.0 fusion.69
  459.1 1.0 fusion.69
  464.0 1.0 fusion.69
  468.9 1.0 fusion.69
  473.8 1.0 fusion.69
  478.7 1.0 fusion.69
  483.7 1.0 fusion.69
  488.6 1.0 fusion.69
  493.5 1.0 fusion.69
  498.4 1.0 fusion.69
  503.3 1.0 fusion.69
  508.2 1.0 fusion.69
  513.2 1.0 fusion.69
  518.1 1.0 fusion.69
  523.0 1.0 fusion.69
  527.9 1.0 fusion.69
  532.8 1.0 fusion.69
  537.8 1.0 fusion.69
  539.1 0.8 copy.51
  540.2 0.8 copy.52
  541.0 112.1 %reduce-scatter.5.cloned.1.call-done = bf16[16,6144]{1,0:T(8,128)(2,1)} async-done(((bf16[512,6144]{1,0:T(8,128)(2,1)}), bf16[16,6144]{1,0:T(8,128)(2,1)}) %reduce-scatter.5.cloned.1.call-update) | async-done | bytes 196624 | tf_op jit(solution)/shard_map/reduce_scatter | solution.py:130
  (106 shorter events, 25.3 us)
Async XLA Ops:
  7.2 4.4 copy-start
  7.2 118.3 %all-gather.10.cloned.1.call-start = ((), (), s32[]{:S(2)}) async-start(), calls=%async_computation.5 | async-start | bytes 4325376 | tf_op jit(solution)/shard_map/all_gather | solution.py:33
  9.0 90.9 %copy-start.11 = (bf16[256,512]{0,1:T(8,128)(2,1)}, bf16[256,512]{0,1:T(8,128)(2,1)S(1)}, u32[]{:S(2)}) copy-start(bf16[256,512]{0,1:T(8,128)(2,1)S(1)} %copy.86) | copy-start | bytes 786436
  12.5 173.6 %all-gather.8.cloned.1.call-start = ((), (), s32[]{:S(2)}) async-start(), calls=%async_computation.2 | async-start | bytes 6488064 | tf_op jit(solution)/shard_map/all_gather | solution.py:116
  13.3 373.1 %all-gather.12.cloned.1.call-start = ((), (), s32[]{:S(2)}) async-start(), calls=%async_computation.6 | async-start | bytes 4325376 | tf_op jit(solution)/shard_map/all_gather | solution.py:33
  13.3 90.3 %collective-permute-start = (bf16[32,6144]{1,0:T(8,128)(2,1)}, bf16[32,6144]{1,0:T(8,128)(2,1)}, u32[]{:S(2)}, u32[]{:S(2)}) collective-permute-start(bf16[32,6144]{1,0:T(8,128)(2,1)} %param.14), channel_id=1, source_target_pairs={{0,1},{1,2},{2,3},{3,4},{4,5},{5,6},{6,7},{7,0},{8,9},{9,10},{10,1... | collective-permute-start | bytes 1179656 | tf_op jit(solution)/shard_map/ppermute | solution.py:18
  18.0 85.6 %collective-permute-start.1 = (bf16[32,6144]{1,0:T(8,128)(2,1)}, bf16[32,6144]{1,0:T(8,128)(2,1)}, u32[]{:S(2)}, u32[]{:S(2)}) collective-permute-start(bf16[32,6144]{1,0:T(8,128)(2,1)} %param.14), channel_id=1, source_target_pairs={{0,7},{1,0},{2,1},{3,2},{4,3},{5,4},{6,5},{7,6},{8,15},{9,8},{10,9... | collective-permute-start | bytes 1179656 | tf_op jit(solution)/shard_map/ppermute | solution.py:21
  99.9 1.2 copy-start.13
  99.9 1.3 copy-start.5
  102.5 15.9 %copy-start.8 = (bf16[4,256,256]{2,1,0:T(8,128)(2,1)}, bf16[4,256,256]{2,1,0:T(8,128)(2,1)S(1)}, u32[]{:S(2)}) copy-start(bf16[4,256,256]{2,1,0:T(8,128)(2,1)S(1)} %fusion.2) | copy-start | bytes 1572868
  103.6 7.4 %collective-permute-start.2 = (bf16[32,6144]{1,0:T(8,128)(2,1)}, bf16[32,6144]{1,0:T(8,128)(2,1)S(1)}, u32[]{:S(2)}, u32[]{:S(2)}) collective-permute-start(bf16[32,6144]{1,0:T(8,128)(2,1)} %collective-permute-done), channel_id=1, source_target_pairs={{0,1},{1,2},{2,3},{3,4},{4,5},{5,6},{6,7},{7,0},{8,9},{9,10},{10,1... | collective-permute-start | bytes 1179656 | tf_op jit(solution)/shard_map/ppermute | solution.py:18
  103.7 7.4 %collective-permute-start.3 = (bf16[32,6144]{1,0:T(8,128)(2,1)}, bf16[32,6144]{1,0:T(8,128)(2,1)S(1)}, u32[]{:S(2)}, u32[]{:S(2)}) collective-permute-start(bf16[32,6144]{1,0:T(8,128)(2,1)} %collective-permute-done.1), channel_id=1, source_target_pairs={{0,7},{1,0},{2,1},{3,2},{4,3},{5,4},{6,5},{7,6},{8,15},{9,8},{10,9... | collective-permute-start | bytes 1179656 | tf_op jit(solution)/shard_map/ppermute | solution.py:21
  111.1 7.2 %collective-permute-start.4 = (bf16[32,6144]{1,0:T(8,128)(2,1)S(1)}, bf16[32,6144]{1,0:T(8,128)(2,1)S(1)}, u32[]{:S(2)}, u32[]{:S(2)}) collective-permute-start(bf16[32,6144]{1,0:T(8,128)(2,1)S(1)} %collective-permute-done.2), channel_id=1, source_target_pairs={{0,1},{1,2},{2,3},{3,4},{4,5},{5,6},{6,7},{7,0},{8,9},{9,10},{10,1... | collective-permute-start | bytes 1179656 | tf_op jit(solution)/shard_map/ppermute | solution.py:18
  111.1 7.3 %collective-permute-start.5 = (bf16[32,6144]{1,0:T(8,128)(2,1)S(1)}, bf16[32,6144]{1,0:T(8,128)(2,1)S(1)}, u32[]{:S(2)}, u32[]{:S(2)}) collective-permute-start(bf16[32,6144]{1,0:T(8,128)(2,1)S(1)} %collective-permute-done.3), channel_id=1, source_target_pairs={{0,7},{1,0},{2,1},{3,2},{4,3},{5,4},{6,5},{7,6},{8,15},{9,8},{10,9... | collective-permute-start | bytes 1179656 | tf_op jit(solution)/shard_map/ppermute | solution.py:21
  113.2 13.1 %copy-start.14 = (s32[256]{0:T(256)S(1)}, s32[256]{0:T(256)}, u32[]{:S(2)}) copy-start(s32[256]{0:T(256)} %param.13) | copy-start | bytes 3076
  118.3 7.2 %collective-permute-start.6 = (bf16[32,6144]{1,0:T(8,128)(2,1)S(1)}, bf16[32,6144]{1,0:T(8,128)(2,1)S(1)}, u32[]{:S(2)}, u32[]{:S(2)}) collective-permute-start(bf16[32,6144]{1,0:T(8,128)(2,1)S(1)} %collective-permute-done.4), channel_id=1, source_target_pairs={{0,1},{1,2},{2,3},{3,4},{4,5},{5,6},{6,7},{7,0},{8,9},{9,10},{10,1... | collective-permute-start | bytes 1179656 | tf_op jit(solution)/shard_map/ppermute | solution.py:18
  186.1 5.5 copy-start.2
  186.1 7.0 %copy-start.6 = (bf16[256,512]{0,1:T(8,128)(2,1)S(1)}, bf16[256,512]{0,1:T(8,128)(2,1)}, u32[]{:S(2)}) copy-start(bf16[256,512]{0,1:T(8,128)(2,1)} %copy.59) | copy-start | bytes 786436
  192.4 0.7 copy-start.3
  194.1 347.0 %reduce-scatter.3.cloned.1.call-start = ((), (), s32[]{:S(2)}) async-start(), calls=%async_computation.3 | async-start | bytes 3538944 | tf_op jit(solution)/shard_map/reduce_scatter | solution.py:117
  200.6 452.5 %reduce-scatter.5.cloned.1.call-start = ((), (), s32[]{:S(2)}) async-start(), calls=%async_computation.4 | async-start | bytes 6488064 | tf_op jit(solution)/shard_map/reduce_scatter | solution.py:130
  206.1 0.9 copy-start.4
  206.1 1.3 copy-start.12
  206.1 1.6 copy-start.1
  206.1 2.7 copy-start.7
  206.1 2.9 copy-start.9
  209.3 330.6 %copy-start.10 = (bf16[256,512]{1,0:T(8,128)(2,1)S(1)}, bf16[256,512]{1,0:T(8,128)(2,1)}, u32[]{:S(2)}) copy-start(bf16[256,512]{1,0:T(8,128)(2,1)} %param.11) | copy-start | bytes 786436
Sparse Core Ops, SparseCore 0:
  12.6 84.8 all-gather.9
  100.1 85.9 all-gather.7
  194.2 192.0 all-gather.11
  389.3 32.1 reduce-scatter.2
  425.9 227.2 reduce-scatter.4
